TPU v7x, 256 devices: a whole 4x4x8 slice. The times are simulated.
256 devices in a mesh: pert: 8 (over z), gene: 32 (over x, y, core).
Axes of the slice: x: 4, y: 4, z: 8, core: 2. Of those that a mesh axis runs over, the one named last changes fastest.
Arguments:
- tensor: bfloat16 [8192, 8, 16384], P('pert', None, 'gene'), may hold values from -2400 to 2400
- pert_factor: bfloat16 [8192, 128], P('pert'), may hold values from -10 to 10
- context_factor: bfloat16 [8, 128], replicated, may hold values from -3 to 3
Outputs:
- gene_factor: bfloat16 [16384, 128], P('gene')
- pert_updated: bfloat16 [8192, 128], P('pert')
All inputs are finite; a program needn't handle non-finite values.
Results may differ from a plain program's by a relative error of at most 0.0042.
Values may be sent and summed in bfloat16 or wider, within the bound.
No kernel may reach another device: no remote copies, remote signals or barrier semaphores. Data moves between devices by JAX's collectives and lax.ppermute only.
A program may use at most 64 MiB of HBM per device.

v0:
```python
import jax
import jax.numpy as jnp
from jax import lax
from jax.sharding import PartitionSpec as P

epsilon = 1e-06


def solve_gram(rhs, gram):
    lower = jnp.linalg.cholesky(gram)
    half = lax.linalg.triangular_solve(lower, rhs, left_side=False, lower=True, transpose_a=True)
    return lax.linalg.triangular_solve(lower, half, left_side=False, lower=True, transpose_a=False)


def raw_gram(solved):
    return jnp.dot(
        solved.T, solved, precision=lax.Precision.HIGHEST, preferred_element_type=jnp.float32
    )


def shards(tensor, pert_factor, context_factor):
    rows_i = tensor.shape[0]
    rows_j = tensor.shape[2]
    n_pert = lax.axis_size("pert")
    n_gene = lax.axis_size("gene")
    context32 = context_factor.astype(jnp.float32)
    gram_b = jnp.dot(context_factor.T, context_factor, preferred_element_type=jnp.float32)
    local_gram = jnp.dot(pert_factor.T, pert_factor, preferred_element_type=jnp.float32)
    gene_count = rows_j * n_gene
    tensor_block = tensor
    partial_sum = jnp.einsum(
        "ikj,ir->kjr", tensor_block, pert_factor, preferred_element_type=jnp.float32
    )
    gram_a, mttkrp_c = lax.psum(
        (local_gram, jnp.sum(partial_sum * context32[:, None, :], axis=0)), "pert"
    )
    solved_c = solve_gram(mttkrp_c, gram_a * gram_b)
    gram_s = lax.psum(raw_gram(solved_c), "gene")
    scale_c = jnp.sqrt(jnp.diagonal(gram_s) / gene_count + epsilon)
    gene_factor = (solved_c / scale_c[None, :]).astype(jnp.bfloat16)
    gram_c = gram_s / (scale_c[:, None] * scale_c[None, :])
    gram_pert_mode = gram_c * gram_b
    pert_count = rows_i * n_pert
    tensor_block = tensor
    partial_sum = jnp.einsum(
        "ikj,jr->ikr", tensor_block, gene_factor, preferred_element_type=jnp.float32
    )
    mttkrp_a = lax.psum(jnp.sum(partial_sum * context32[None, :, :], axis=1), "gene")
    solved_a = solve_gram(mttkrp_a, gram_pert_mode)
    squares_a = lax.psum(jnp.sum(solved_a * solved_a, axis=0), "pert")
    scale_a = jnp.sqrt(squares_a / pert_count + epsilon)
    pert_updated = (solved_a / scale_a[None, :]).astype(jnp.bfloat16)
    return (gene_factor, pert_updated)


def solution(mesh):
    return jax.shard_map(
        shards,
        mesh=mesh,
        in_specs=(P("pert", None, "gene"), P("pert", None), P()),
        out_specs=(P("gene", None), P("pert", None)),
        check_vma=False,
    )
```

profile of v0, /device:TPU:6, one launch (start us, length us, event | category | flops | bytes accessed | tf_op | source)
XLA Modules:
  0.0 397.8 jit_solution(13535459443830926320)
XLA Ops:
  7.2 0.7 convert_element_type.9
  8.1 0.9 fusion.24
  9.0 13.0 %multiply_reduce_fusion = f32[512,128]{1,0:T(8,128)} fusion(bf16[1024,8,512]{2,1,0:T(8,128)(2,1)} %param.4, f32[8,128]{1,0:T(8,128)S(1)} %convert_element_type.9, bf16[1024,128]{1,0:T(8,128)(2,1)S(1)} %copy-done), kind=kOutput, calls=%fused_computation.7 | convolution fusion | flops 1074724864 | bytes 8916992 | tf_op jit(solution)/shard_map/ikj,ir->kjr/dot_general | solution.py:31
  22.3 76.0 %all-reduce.9.cloned.1.call-done = (f32[512,128]{1,0:T(8,128)}, f32[128,128]{0,1:T(8,128)}) async-done(((f32[512,128]{1,0:T(8,128)}, f32[128,128]{0,1:T(8,128)}), (f32[512,128]{1,0:T(8,128)}, f32[128,128]{0,1:T(8,128)})) %all-reduce.9.cloned.1.call-update) | async-done | bytes 327696 | tf_op jit(solution)/shard_map/psum | solution.py:34
  98.3 1.1 fusion.23
  99.5 11.7 %cholesky.44 = f32[128,128]{1,0:T(8,128)S(1)} custom-call(f32[128,128]{1,0:T(8,128)S(1)} %fusion.22), custom_call_target="Cholesky" | custom-call | tf_op jit(solution)/shard_map/jit(cholesky)/cholesky | solution.py:10
  111.2 0.6 compare_reduce_fusion.1
  111.9 0.7 fusion.11
  112.5 9.8 %custom-call.12 = f32[1,128,128]{1,2,0:T(8,128)S(1)} custom-call(f32[1,128,128]{2,1,0:T(8,128)S(1)} %fusion.11), custom_call_target="InvertDiagBlocksLowerTriangular" | custom-call | tf_op jit(solution)/shard_map/triangular_solve | solution.py:11
  122.3 1.3 fusion.20
  124.0 1.2 fusion.25
  125.6 104.5 %all-reduce.5.cloned.1.call-done = f32[128,128]{0,1:T(8,128)} async-done(((f32[128,128]{0,1:T(8,128)}), f32[128,128]{0,1:T(8,128)}) %all-reduce.5.cloned.1.call-update) | async-done | bytes 65552 | tf_op jit(solution)/shard_map/psum | solution.py:38
  230.1 1.9 gather_fusion
  232.1 1.0 divide_multiply_fusion
  233.2 11.7 %cholesky.55 = f32[128,128]{1,0:T(8,128)S(1)} custom-call(f32[128,128]{1,0:T(8,128)S(1)} %fusion.17), custom_call_target="Cholesky" | custom-call | tf_op jit(solution)/shard_map/jit(cholesky)/cholesky | solution.py:10
  244.9 9.5 %fusion.4 = f32[1024,128]{0,1:T(8,128)S(1)} fusion(bf16[1024,8,512]{2,1,0:T(8,128)(2,1)} %param.4, f32[8,128]{1,0:T(8,128)S(1)} %convert_element_type.9, bf16[512,128]{1,0:T(8,128)(2,1)S(1)} %divide_convert_fusion.1), kind=kOutput, calls=%fused_computation.6 | convolution fusion | flops 1075707904 | bytes 9048064 | tf_op jit(solution)/shard_map/ikj,jr->ikr/dot_general | solution.py:45
  254.4 1.0 copy.34
  255.4 0.6 compare_reduce_fusion
  256.1 0.7 fusion.12
  256.7 9.8 %custom-call.13 = f32[1,128,128]{1,2,0:T(8,128)S(1)} custom-call(f32[1,128,128]{2,1,0:T(8,128)S(1)} %fusion.12), custom_call_target="InvertDiagBlocksLowerTriangular" | custom-call | tf_op jit(solution)/shard_map/triangular_solve | solution.py:11
  266.6 104.2 %all-reduce.7.cloned.1.call-done = f32[1024,128]{1,0:T(8,128)} async-done(((f32[1024,128]{1,0:T(8,128)}), f32[1024,128]{1,0:T(8,128)}) %all-reduce.7.cloned.1.call-update) | async-done | bytes 524304 | tf_op jit(solution)/shard_map/psum | solution.py:48
  370.8 1.6 fusion.15
  373.0 17.5 %psum.39 = f32[128]{0:T(128)S(1)} all-reduce(f32[128]{0:T(128)S(1)} %get-tuple-element.7), channel_id=1, replica_groups=mesh['pert'=8,'gene'=32] {'pert'}, use_global_device_ids=true, to_apply=%region_9.11 | all-reduce | flops 128 | bytes 1024 | tf_op jit(solution)/shard_map/psum | solution.py:50
  390.5 0.8 divide_convert_fusion
  (24 shorter events, 2.1 us)
Async XLA Ops:
  7.2 1.0 copy-start
  7.2 91.1 %copy-start.2 = (bf16[8,128]{1,0:T(8,128)(2,1)S(1)}, bf16[8,128]{1,0:T(8,128)(2,1)}, u32[]{:S(2)}) copy-start(bf16[8,128]{1,0:T(8,128)(2,1)} %param.6) | copy-start | bytes 6148
  7.2 91.1 %all-reduce.9.cloned.1.call-start = ((), (), s32[]{:S(2)}) async-start(), calls=%async_computation.2 | async-start | bytes 655360 | tf_op jit(solution)/shard_map/psum | solution.py:34
  22.0 208.1 %all-reduce.5.cloned.1.call-start = ((), (), s32[]{:S(2)}) async-start(), calls=%async_computation | async-start | bytes 131072 | tf_op jit(solution)/shard_map/psum | solution.py:38
  125.3 245.5 %all-reduce.7.cloned.1.call-start = ((), (), s32[]{:S(2)}) async-start(), calls=%async_computation.1 | async-start | bytes 1048576 | tf_op jit(solution)/shard_map/psum | solution.py:48
  232.1 140.9 %copy-start.1 = (bf16[512,128]{1,0:T(8,128)(2,1)}, bf16[512,128]{1,0:T(8,128)(2,1)S(1)}, u32[]{:S(2)}) copy-start(bf16[512,128]{1,0:T(8,128)(2,1)S(1)} %divide_convert_fusion.1) | copy-start | bytes 393220
Sparse Core Ops, SparseCore 0:
  22.1 76.1 all-reduce.8
  125.4 104.6 all-reduce.4
  255.6 115.1 all-reduce.6
where the time goes:
time: 398 us
  waiting for transfers between devices  285 us (72%)
  other arithmetic  48.2 us (12%)
  matrix products  29.5 us (7%)
  blocking collectives  17.5 us (4%)
  between operations  13.9 us (3%)
    psum x1, waiting for transfers between devices, shards(): gram_s = lax.psum(raw_gram(solved_c), 'gene')  105 us
    psum x1, waiting for transfers between devices, shards(): lax.psum(jnp.sum(partial_sum * context32[None, :, :], axis=1), 'gene')  104 us
    psum x1, waiting for transfers between devices, shards(): lax.psum((local_gram, jnp.sum(partial_sum * context32[:, None, :], axis=0...  76 us
    another operation x6, other arithmetic, solve_gram(): lower = jnp.linalg.cholesky(gram)  24.8 us
    another operation x4, other arithmetic, solve_gram(): lax.linalg.triangular_solve(lower, rhs, left_side=False, lower=True, tran...  20.9 us
    psum x1, blocking collectives, shards(): squares_a = lax.psum(jnp.sum(solved_a * solved_a, axis=0), 'pert')  17.5 us
    dot_general x1, matrix products, shards(): jnp.einsum('ikj,ir->kjr', tensor_block, pert_factor, preferred_element_ty...  13 us
    dot_general x1, matrix products, shards(): jnp.einsum('ikj,jr->ikr', tensor_block, gene_factor, preferred_element_ty...  9.45 us
  transfers between devices with their start and end apart: 3, of which 3 were waited for; matrix products, arithmetic and copies ran while one was open for 3% of the time, Pallas kernels for 0%

commit v1 on v0

--- a/solution.py
+++ b/solution.py
@@ -45,7 +45,9 @@
     partial_sum = jnp.einsum(
         "ikj,jr->ikr", tensor_block, gene_factor, preferred_element_type=jnp.float32
     )
-    mttkrp_a = lax.psum(jnp.sum(partial_sum * context32[None, :, :], axis=1), "gene")
+    mttkrp_a = jnp.sum(
+        lax.all_gather(jnp.sum(partial_sum * context32[None, :, :], axis=1), "gene"), axis=0
+    )
     solved_a = solve_gram(mttkrp_a, gram_pert_mode)
     squares_a = lax.psum(jnp.sum(solved_a * solved_a, axis=0), "pert")
     scale_a = jnp.sqrt(squares_a / pert_count + epsilon)

time: 398 us -> 381 us (0.957); the launches traced: 398 us -> 374 us
  waiting for transfers between devices: 285 us -> 235 us
  local copies, waits for them, and re-layouts: 3.32 us -> 20.1 us
  other arithmetic: 48.2 us -> 56.6 us
    psum x1 -> x0, waiting for transfers between devices: 104 us -> none  [shards(): lax.psum(jnp.sum(partial_sum * context32[None, :, :], axis=1), 'gene')]
    all_gather x0 -> x1, waiting for transfers between devices: none -> 54.6 us  [shards(): lax.all_gather(jnp.sum(partial_sum * context32[None, :, :], axis=1), 'gene')]
    unnamed x7 -> x9, local copies, waits for them, and re-layouts: 1.2 us -> 17.9 us
    reduce_sum x0 -> x1, other arithmetic: none -> 9.05 us  [shards(): jnp.sum(lax.all_gather(jnp.sum(partial_sum * context32[None, :, :], axis=...]
  transfers between devices with their start and end apart: 3 -> 3, of which waited for: 3 -> 3; matrix products, arithmetic and copies ran while one was open for 3% -> 6% of each run, Pallas kernels for 0% -> 0%
where the time goes in v1:
time: 381 us; the launch traced here: 374 us
  waiting for transfers between devices  235 us (62%)
  other arithmetic  56.6 us (15%)
  matrix products  29.7 us (8%)
  local copies, waits for them, and re-layouts  20.1 us (5%)
  blocking collectives  17.5 us (5%)
  between operations  14.1 us (4%)
    psum x1, waiting for transfers between devices, shards(): gram_s = lax.psum(raw_gram(solved_c), 'gene')  105 us
    psum x1, waiting for transfers between devices, shards(): lax.psum((local_gram, jnp.sum(partial_sum * context32[:, None, :], axis=0...  75.8 us
    all_gather x1, waiting for transfers between devices, shards(): lax.all_gather(jnp.sum(partial_sum * context32[None, :, :], axis=1), 'gene')  54.6 us
    another operation x6, other arithmetic, solve_gram(): lower = jnp.linalg.cholesky(gram)  24.8 us
    another operation x4, other arithmetic, solve_gram(): lax.linalg.triangular_solve(lower, rhs, left_side=False, lower=True, tran...  21.1 us
    unnamed x9, local copies, waits for them, and re-layouts  17.9 us
    psum x1, blocking collectives, shards(): squares_a = lax.psum(jnp.sum(solved_a * solved_a, axis=0), 'pert')  17.5 us
    dot_general x1, matrix products, shards(): jnp.einsum('ikj,ir->kjr', tensor_block, pert_factor, preferred_element_ty...  13 us
  transfers between devices with their start and end apart: 3, of which 3 were waited for; matrix products, arithmetic and copies ran while one was open for 6% of the time, Pallas kernels for 0%

profile of v1, /device:TPU:6, one launch (start us, length us, event | category | flops | bytes accessed | tf_op | source)
XLA Modules:
  0.0 373.7 jit_solution(12850135537966334535)
XLA Ops:
  7.2 0.7 convert_element_type.9
  8.1 0.9 fusion.24
  9.0 13.0 %multiply_reduce_fusion = f32[512,128]{1,0:T(8,128)} fusion(bf16[1024,8,512]{2,1,0:T(8,128)(2,1)} %param.4, f32[8,128]{1,0:T(8,128)S(1)} %convert_element_type.9, bf16[1024,128]{1,0:T(8,128)(2,1)S(1)} %copy-done), kind=kOutput, calls=%fused_computation.8 | convolution fusion | flops 1074724864 | bytes 8916992 | tf_op jit(solution)/shard_map/ikj,ir->kjr/dot_general | solution.py:31
  22.5 75.8 %all-reduce.6.cloned.1.call-done = (f32[512,128]{1,0:T(8,128)}, f32[128,128]{0,1:T(8,128)}) async-done(((f32[512,128]{1,0:T(8,128)}, f32[128,128]{0,1:T(8,128)}), (f32[512,128]{1,0:T(8,128)}, f32[128,128]{0,1:T(8,128)})) %all-reduce.6.cloned.1.call-update) | async-done | bytes 327696 | tf_op jit(solution)/shard_map/psum | solution.py:34
  98.3 1.1 fusion.23
  99.5 11.7 %cholesky.44 = f32[128,128]{1,0:T(8,128)S(1)} custom-call(f32[128,128]{1,0:T(8,128)S(1)} %fusion.22), custom_call_target="Cholesky" | custom-call | tf_op jit(solution)/shard_map/jit(cholesky)/cholesky | solution.py:10
  111.2 0.6 compare_reduce_fusion.1
  111.9 0.7 fusion.11
  112.5 9.8 %custom-call.12 = f32[1,128,128]{1,2,0:T(8,128)S(1)} custom-call(f32[1,128,128]{2,1,0:T(8,128)S(1)} %fusion.11), custom_call_target="InvertDiagBlocksLowerTriangular" | custom-call | tf_op jit(solution)/shard_map/triangular_solve | solution.py:11
  122.3 1.3 fusion.20
  124.0 1.2 fusion.25
  125.5 104.6 %all-reduce.4.cloned.1.call-done = f32[128,128]{0,1:T(8,128)} async-done(((f32[128,128]{0,1:T(8,128)}), f32[128,128]{0,1:T(8,128)}) %all-reduce.4.cloned.1.call-update) | async-done | bytes 65552 | tf_op jit(solution)/shard_map/psum | solution.py:38
  230.1 2.0 gather_fusion
  232.2 10.2 %fusion.4 = f32[1024,128]{0,1:T(8,128)} fusion(bf16[1024,8,512]{2,1,0:T(8,128)(2,1)} %param.4, f32[8,128]{1,0:T(8,128)S(1)} %convert_element_type.9, bf16[512,128]{1,0:T(8,128)(2,1)S(1)} %divide_convert_fusion.1), kind=kOutput, calls=%fused_computation.7 | convolution fusion | flops 1075707904 | bytes 9048064 | tf_op jit(solution)/shard_map/ikj,jr->ikr/dot_general | solution.py:45
  242.7 11.7 %cholesky.55 = f32[128,128]{1,0:T(8,128)S(1)} custom-call(f32[128,128]{1,0:T(8,128)S(1)} %fusion.17), custom_call_target="Cholesky" | custom-call | tf_op jit(solution)/shard_map/jit(cholesky)/cholesky | solution.py:10
  254.4 0.6 compare_reduce_fusion
  255.1 0.7 fusion.12
  255.7 10.0 %custom-call.13 = f32[1,128,128]{1,2,0:T(8,128)S(1)} custom-call(f32[1,128,128]{2,1,0:T(8,128)S(1)} %fusion.12), custom_call_target="InvertDiagBlocksLowerTriangular" | custom-call | tf_op jit(solution)/shard_map/triangular_solve | solution.py:11
  265.7 54.6 %all-gather.3.cloned.1.call-done = f32[32768,128]{0,1:T(8,128)} async-done(((f32[1024,128]{0,1:T(8,128)}), f32[32768,128]{0,1:T(8,128)}) %all-gather.3.cloned.1.call-update) | async-done | bytes 16777232 | tf_op jit(solution)/shard_map/all_gather | solution.py:49
  320.4 17.7 %copy.44 = f32[16,8,32,1024]{3,2,1,0:T(8,128)} copy(f32[16,8,32,1024]{3,1,2,0:T(8,128)} %bitcast.51) | data formatting | bytes 33554432
  338.0 9.0 %bitcast_reduce_fusion = f32[1024,128]{0,1:T(8,128)S(1)} fusion(f32[16,8,32,1024]{3,2,1,0:T(8,128)} %copy.44), kind=kLoop, calls=%fused_computation.1 | loop fusion | flops 4063232 | bytes 17301504 | tf_op jit(solution)/shard_map/reduce_sum | solution.py:48
  347.1 1.0 fusion.15
  348.7 17.5 %psum.31 = f32[128]{0:T(128)S(1)} all-reduce(f32[128]{0:T(128)S(1)} %get-tuple-element.7), channel_id=1, replica_groups=mesh['pert'=8,'gene'=32] {'pert'}, use_global_device_ids=true, to_apply=%region_9.11 | all-reduce | flops 128 | bytes 1024 | tf_op jit(solution)/shard_map/psum | solution.py:52
  366.2 0.8 divide_convert_fusion
  (27 shorter events, 2.4 us)
Async XLA Ops:
  7.2 1.0 copy-start
  7.2 91.1 %copy-start.3 = (bf16[8,128]{1,0:T(8,128)(2,1)S(1)}, bf16[8,128]{1,0:T(8,128)(2,1)}, u32[]{:S(2)}) copy-start(bf16[8,128]{1,0:T(8,128)(2,1)} %param.6) | copy-start | bytes 6148
  7.2 91.1 %all-reduce.6.cloned.1.call-start = ((), (), s32[]{:S(2)}) async-start(), calls=%async_computation.2 | async-start | bytes 655360 | tf_op jit(solution)/shard_map/psum | solution.py:34
  22.0 208.1 %all-reduce.4.cloned.1.call-start = ((), (), s32[]{:S(2)}) async-start(), calls=%async_computation | async-start | bytes 131072 | tf_op jit(solution)/shard_map/psum | solution.py:38
  125.3 195.1 %all-gather.3.cloned.1.call-start = ((), (), s32[]{:S(2)}) async-start(), calls=%async_computation.1 | async-start | bytes 17301504 | tf_op jit(solution)/shard_map/all_gather | solution.py:49
  230.1 12.4 %copy-start.1 = (f32[128,128]{0,1:T(8,128)S(1)}, f32[128,128]{0,1:T(8,128)}, u32[]{:S(2)}) copy-start(f32[128,128]{0,1:T(8,128)} %all-reduce.4.cloned.1.call-done) | copy-start | bytes 196612
  232.2 105.9 %copy-start.2 = (bf16[512,128]{1,0:T(8,128)(2,1)}, bf16[512,128]{1,0:T(8,128)(2,1)S(1)}, u32[]{:S(2)}) copy-start(bf16[512,128]{1,0:T(8,128)(2,1)S(1)} %divide_convert_fusion.1) | copy-start | bytes 393220
Sparse Core Ops, SparseCore 0:
  22.1 76.1 all-reduce.5
  125.4 104.6 all-reduce.3
  242.6 77.7 all-gather.2
